TPU v7x, 32 devices: a whole 2x2x4 slice. The times are simulated.
32 devices in a mesh: tm: 4 (over z), lon: 8 (over y, x, core).
Axes of the slice: x: 2, y: 2, z: 4, core: 2. Of those that a mesh axis runs over, the one named last changes fastest.
Arguments:
- rhs_state: float32 [4, 3, 1024, 2048], P('tm', None, None, 'lon'), may hold values from -30 to 30
- innovations: float32 [4, 8192], P('tm', 'lon'), may hold values from -6 to 6
- trajectory: bfloat16 [4, 2, 3, 1024, 2048], P('tm', None, None, None, 'lon'), may hold values from -1 to 1.5, as said below
- model_var: float32 [4, 3, 1024, 2048], P('tm', None, None, 'lon'), may hold values from 0.2 to 2
- obs_var: float32 [4, 8192], P('tm', 'lon'), may hold values from 0.2 to 2
- obs_index: int32 [4, 8192], P('tm', 'lon'), may hold values from 0 to 786431, as said below
- control_rhs: float32 [4, 3, 1024, 2048], P('tm', None, None, 'lon'), may hold values from -30 to 30
Outputs:
- multiplier_out: float32 [4, 3, 1024, 2048], P('tm', None, None, 'lon')
- obs_dual_out: float32 [4, 8192], P('tm', 'lon')
- increment_out: float32 [4, 3, 1024, 2048], P('tm', None, None, 'lon')
Inputs may be any that keep to these rules, and one draw needn't show every extreme that they name: obs_index[k, j] = (field 1024 + row) * 256 + column with field 0 to 2, row 0 to 1023 and column 0 to 255 within the band j // 1024; an index may repeat. Field 0 of trajectory is the depth, fields 1 and 2 the winds.
All inputs are finite; a program needn't handle non-finite values.
Results may differ from a plain program's by a relative error of at most 0.0003.
Values sent between devices are 32-bit elements; how exact they have to be, the bound alone decides.
No kernel may reach another device: no remote copies, remote signals or barrier semaphores. Data moves between devices by JAX's collectives and lax.ppermute only.
A program may use at most 192 MiB of HBM per device.

v0:
```python
import jax
import jax.numpy as jnp
from jax import lax
from jax.sharding import PartitionSpec as P

courant = 0.25
coriolis = 0.2


def passed_along(block, axis, distance):
    devices = range(lax.axis_size(axis))
    route = [(i - distance, i) for i in devices if i - distance in devices]
    return lax.ppermute(block, axis, route)


def with_halo(shard, sides, width):
    for axis, dim in sides:
        peers, length = (lax.axis_size(axis), shard.shape[dim])
        up = [(i, (i + 1) % peers) for i in range(peers)]
        down = [(j, i) for i, j in up]
        last = lax.slice_in_dim(shard, length - width, length, axis=dim)
        first = lax.slice_in_dim(shard, 0, width, axis=dim)
        before = lax.ppermute(last, axis, up)
        after = lax.ppermute(first, axis, down)
        shard = jnp.concatenate([before, shard, after], axis=dim)
    return shard


def coriolis_rows(rows):
    position = jnp.arange(rows, dtype=jnp.float32)
    return (coriolis * ((2.0 * position + 1.0) / rows - 1.0))[:, None]


def centered_x(extended):
    return 0.5 * (extended[:, :, 2:] - extended[:, :, :-2])


def walled_y(field):
    padded = jnp.pad(field, ((0, 0), (1, 1), (0, 0)))
    return 0.5 * (padded[:, 2:, :] - padded[:, :-2, :])


def tangent_step(current, x_diffs, traj_step, rotation):
    mean_depth = traj_step[0].astype(jnp.float32)
    mean_east = traj_step[1].astype(jnp.float32)
    mean_north = traj_step[2].astype(jnp.float32)
    y_diffs = walled_y(current)
    height = current[0]
    east_wind = current[1]
    north_wind = current[2]
    new_height = height - courant * (
        mean_depth * (x_diffs[1] + y_diffs[2]) + mean_east * x_diffs[0] + mean_north * y_diffs[0]
    )
    new_east = (
        east_wind
        - courant * (x_diffs[0] + mean_east * x_diffs[1] + mean_north * y_diffs[1])
        + rotation * north_wind
    )
    new_north = (
        north_wind
        - courant * (y_diffs[0] + mean_east * x_diffs[2] + mean_north * y_diffs[2])
        - rotation * east_wind
    )
    return jnp.stack([new_height, new_east, new_north])


def east_fluxes(adjoint, traj_step):
    mean_depth = traj_step[0].astype(jnp.float32)
    mean_east = traj_step[1].astype(jnp.float32)
    return jnp.stack(
        [
            mean_east * adjoint[0] + adjoint[1],
            mean_depth * adjoint[0] + mean_east * adjoint[1],
            mean_east * adjoint[2],
        ]
    )


def north_fluxes(adjoint, traj_step):
    mean_depth = traj_step[0].astype(jnp.float32)
    mean_north = traj_step[2].astype(jnp.float32)
    return jnp.stack(
        [
            mean_north * adjoint[0] + adjoint[2],
            mean_north * adjoint[1],
            mean_depth * adjoint[0] + mean_north * adjoint[2],
        ]
    )


def adjoint_step(adjoint, x_diffs, traj_step, rotation):
    y_diffs = walled_y(north_fluxes(adjoint, traj_step))
    new_height = adjoint[0] + courant * (x_diffs[0] + y_diffs[0])
    new_east = adjoint[1] + courant * (x_diffs[1] + y_diffs[1]) - rotation * adjoint[2]
    new_north = adjoint[2] + courant * (x_diffs[2] + y_diffs[2]) + rotation * adjoint[1]
    return jnp.stack([new_height, new_east, new_north])


def apply_saddle(vector, traj_dev, model_part, obs_part, local_index, rotation):
    multiplier, obs_dual, increment = vector
    steps_total = traj_dev.shape[0]
    later = passed_along(multiplier, "tm", -1)
    current = increment
    adjoint = later
    for step_number in range(steps_total):
        extended = with_halo(current, (("lon", 2),), 1)
        current = tangent_step(current, centered_x(extended), traj_dev[step_number], rotation)
    for step_number in reversed(range(steps_total)):
        fluxes = east_fluxes(adjoint, traj_dev[step_number])
        extended = with_halo(fluxes, (("lon", 2),), 1)
        adjoint = adjoint_step(adjoint, centered_x(extended), traj_dev[step_number], rotation)
    earlier = passed_along(current, "tm", 1)
    flat_inc = increment.reshape(-1)
    observed = flat_inc[local_index]
    spread = jnp.zeros_like(flat_inc).at[local_index].add(obs_dual).reshape(increment.shape)
    row_one = model_part * multiplier + increment - earlier
    row_two = obs_part * obs_dual + observed
    row_three = multiplier - adjoint + spread
    return (row_one, row_two, row_three)


def precondition(vector, model_part, obs_part):
    return (vector[2], vector[1] / obs_part, vector[0] - model_part * vector[2])


def local_product(first_vec, second_vec):
    return (
        jnp.sum(first_vec[0] * second_vec[0])
        + jnp.sum(first_vec[1] * second_vec[1])
        + jnp.sum(first_vec[2] * second_vec[2])
    )


def scaled(vector, factor):
    return tuple((block * factor for block in vector))


def minus_scaled(vector, other, factor):
    return tuple((block - factor * piece for block, piece in zip(vector, other)))


def orthogonalize(image, basis_list):
    coef_list = []
    for vector in basis_list:
        coef_value = lax.psum(local_product(vector, image), ("tm", "lon"))
        image = minus_scaled(image, vector, coef_value)
        coef_list.append(coef_value)
    remain = lax.psum(local_product(image, image), ("tm", "lon"))
    return (image, coef_list, jnp.sqrt(remain))


def shards(rhs_state, innovations, trajectory, model_var, obs_var, obs_index, control_rhs):
    local_index = obs_index[0]
    rotation = coriolis_rows(rhs_state.shape[2])
    traj_dev = trajectory[0]
    model_part = model_var[0]
    obs_part = obs_var[0]
    start = (rhs_state[0], innovations[0], control_rhs[0])
    start_square = lax.psum(local_product(start, start), ("tm", "lon"))
    beta = jnp.sqrt(start_square)
    basis_zero = scaled(start, 1.0 / beta)
    precond_zero = precondition(basis_zero, model_part, obs_part)
    image = apply_saddle(precond_zero, traj_dev, model_part, obs_part, local_index, rotation)
    image, coef_first, below_first = orthogonalize(image, [basis_zero])
    diag_first = coef_first[0]
    basis_one = scaled(image, 1.0 / below_first)
    precond_one = precondition(basis_one, model_part, obs_part)
    image = apply_saddle(precond_one, traj_dev, model_part, obs_part, local_index, rotation)
    image, coef_second, below_second = orthogonalize(image, [basis_zero, basis_one])
    upper_second = coef_second[0]
    diag_second = coef_second[1]
    gram_zero = diag_first * diag_first + below_first * below_first
    gram_cross = diag_first * upper_second + below_first * diag_second
    gram_one = upper_second * upper_second + diag_second * diag_second + below_second * below_second
    target_zero = beta * diag_first
    target_one = beta * upper_second
    determinant = gram_zero * gram_one - gram_cross * gram_cross
    weight_zero = (gram_one * target_zero - gram_cross * target_one) / determinant
    weight_one = (gram_zero * target_one - gram_cross * target_zero) / determinant
    result = tuple(
        (
            block_a * weight_zero + block_b * weight_one
            for block_a, block_b in zip(precond_zero, precond_one)
        )
    )
    return (result[0][None], result[1][None], result[2][None])


def solution(mesh):
    in_specs = (
        P("tm", None, None, "lon"),
        P("tm", "lon"),
        P("tm", None, None, None, "lon"),
        P("tm", None, None, "lon"),
        P("tm", "lon"),
        P("tm", "lon"),
        P("tm", None, None, "lon"),
    )
    out_specs = (P("tm", None, None, "lon"), P("tm", "lon"), P("tm", None, None, "lon"))
    return jax.shard_map(shards, mesh=mesh, in_specs=in_specs, out_specs=out_specs, check_vma=False)
```

profile of v0, /device:TPU:0, one launch (start us, length us, event | category | flops | bytes accessed | tf_op | source)
XLA Modules:
  0.0 725.3 jit_solution(345166367682195843)
XLA Ops:
  8.8 42.0 %psum.42 = f32[]{:T(128)} all-reduce(f32[]{:T(128)S(6)} %add.566), channel_id=1, replica_groups=mesh['tm'=4,'lon'=8] {'tm','lon'}, use_global_device_ids=true, to_apply=%region_3.0 | all-reduce | flops 1 | bytes 8 | tf_op jit(solution)/shard_map/psum | solution.py:159
  51.5 7.8 %bitcast_subtract_fusion = (f32[3,1024,256]{2,1,0:T(8,128)S(1)}, f32[3,1024,256]{2,1,0:T(8,128)}, f32[1,3,1024,256]{3,2,1,0:T(8,128)S(1)}, f32[1,3,1024,256]{3,2,1,0:T(8,128)}) fusion(f32[1,3,1024,256]{3,2,1,0:T(8,128)} %param.10, f32[1,3,1024,256]{3,2,1,0:T(8,128)} %param.7, f32[]{:T(128)S(6)} %div.60, f32[1,3,1024,256]{3,2,1,0:T(8,128)} %param.13), kind=kLoop, calls=%fused_computation.149 | loop fusion | flops 3145728 | bytes 22020100 | tf_op jit(solution)/shard_map/sub | solution.py:123
  82.2 8.1 %subtract_multiply_fusion.4 = (f32[3,1024,256]{2,1,0:T(8,128)S(1)}, f32[3,1024,256]{2,1,0:T(8,128)S(1)}) fusion(f32[3,1024,256]{2,1,0:T(8,128)} %copy-done.19, f32[3,1024,1]{2,1,0:T(8,128)} %copy.32, f32[3,1024,1]{2,1,0:T(8,128)} %copy.30), kind=kLoop, calls=%fused_computation.171 | loop fusion | flops 4718592 | bytes 9461760 | tf_op jit(solution)/shard_map/mul | solution.py:40
  119.5 20.1 %collective-permute-done = f32[3,1024,256]{2,1,0:T(8,128)} collective-permute-done((f32[3,1024,256]{2,1,0:T(8,128)}, f32[3,1024,256]{2,1,0:T(8,128)}, u32[]{:S(2)}, u32[]{:S(2)}) %collective-permute-start) | collective-permute-done | bytes 3145760 | tf_op jit(solution)/shard_map/ppermute | solution.py:13
  160.5 6.8 fusion.20
  184.4 12.5 %gather_fusion = f32[1024]{0:T(1024)S(1)} fusion(f32[786432]{0:T(1024)} %multiply_subtract_fusion.2, s32[1024]{0:T(1024)S(1)} %broadcast_clamp_fusion), kind=kCustom, calls=%fused_computation | custom fusion | bytes 12288 | tf_op jit(solution)/shard_map/gather | solution.py:114
  197.6 7.8 %scatter_custom_fusion = f32[786432]{0:T(1024)} fusion(s32[1024]{0:T(1024)S(1)} %bitcast.166, f32[1024]{0:T(1024)S(1)} %get-tuple-element.25, f32[]{:T(128)} %constant.11.clone.1), kind=kCustom, calls=%fused_computation.187 | custom fusion | flops 1024 | bytes 3145732 | tf_op jit(solution)/shard_map/scatter-add | solution.py:115
  228.0 6.6 fusion.17
  241.6 8.9 %collective-permute-done.9 = f32[3,1024,256]{2,1,0:T(8,128)} collective-permute-done((f32[3,1024,256]{2,1,0:T(8,128)}, f32[3,1024,256]{2,1,0:T(8,128)}, u32[]{:S(2)}, u32[]{:S(2)}) %collective-permute-start.9) | collective-permute-done | bytes 3145760 | tf_op jit(solution)/shard_map/ppermute | solution.py:13
  261.1 40.6 %psum.43 = f32[]{:T(128)} all-reduce(f32[]{:T(128)S(6)} %add.611), channel_id=1, replica_groups=mesh['tm'=4,'lon'=8] {'tm','lon'}, use_global_device_ids=true, to_apply=%region_8.9 | all-reduce | flops 1 | bytes 8 | tf_op jit(solution)/shard_map/psum | solution.py:145
  303.0 7.8 %multiply_reduce_fusion.5 = (f32[]{:T(128)}, f32[786432]{0:T(1024)}) fusion(f32[786432]{0:T(1024)} %bitcast.141, f32[]{:T(128)} %psum.43, f32[786432]{0:T(1024)} %scatter_custom_fusion, f32[786432]{0:T(1024)} %bitcast.153), kind=kLoop, calls=%fused_computation.164 | loop fusion | flops 4718591 | bytes 12582920 | tf_op jit(solution)/shard_map/reduce_sum | solution.py:130
  318.4 39.2 %psum.44 = f32[]{:T(128)} all-reduce(f32[]{:T(128)S(6)} %add.614), channel_id=1, replica_groups=mesh['tm'=4,'lon'=8] {'tm','lon'}, use_global_device_ids=true, to_apply=%region_12.13 | all-reduce | flops 1 | bytes 8 | tf_op jit(solution)/shard_map/psum | solution.py:148
  358.4 9.1 %multiply_subtract_fusion.3 = (f32[3,1024,256]{2,1,0:T(8,128)S(1)}, f32[3,1024,256]{2,1,0:T(8,128)}) fusion(f32[3,1024,256]{2,1,0:T(8,128)} %get-tuple-element.23, f32[]{:T(128)S(6)} %div.64, f32[1,3,1024,256]{3,2,1,0:T(8,128)} %param.10, f32[]{:T(128)} %psum.43, f32[3,1024,256]{2,1,0:T(8,128)} %reshape.519, f32[1,1024,256]{2,1,0:T(8,128)} %copy-done.41, ...), kind=kLoop, calls=%fused_computation.176 | loop fusion | flops 7864320 | bytes 22020104 | tf_op jit(solution)/shard_map/sub | solution.py:123
  381.6 8.2 %subtract_multiply_fusion.1 = (f32[3,1024,256]{2,1,0:T(8,128)S(1)}, f32[3,1024,256]{2,1,0:T(8,128)S(1)}) fusion(f32[3,1024,256]{2,1,0:T(8,128)} %copy-done, f32[3,1024,1]{2,1,0:T(8,128)} %copy.40, f32[3,1024,1]{2,1,0:T(8,128)} %copy.38), kind=kLoop, calls=%fused_computation.162 | loop fusion | flops 4718592 | bytes 9461760 | tf_op jit(solution)/shard_map/mul | solution.py:40
  407.9 6.6 fusion.8
  416.8 22.2 %collective-permute-done.15 = f32[3,1024,256]{2,1,0:T(8,128)} collective-permute-done((f32[3,1024,256]{2,1,0:T(8,128)}, f32[3,1024,256]{2,1,0:T(8,128)}, u32[]{:S(2)}, u32[]{:S(2)}) %collective-permute-start.15) | collective-permute-done | bytes 3145760 | tf_op jit(solution)/shard_map/ppermute | solution.py:13
  458.5 6.5 fusion.6
  491.7 12.5 %gather_fusion.1 = f32[1024]{0:T(1024)S(1)} fusion(f32[786432]{0:T(1024)} %bitcast.147, s32[1024]{0:T(1024)S(1)} %broadcast_clamp_fusion), kind=kCustom, calls=%fused_computation.1 | custom fusion | bytes 12288 | tf_op jit(solution)/shard_map/gather | solution.py:114
  504.8 7.8 %scatter_custom_fusion.1 = f32[786432]{0:T(1024)} fusion(s32[1024]{0:T(1024)S(1)} %bitcast.167, f32[1024]{0:T(1024)S(1)} %get-tuple-element.13, f32[]{:T(128)} %constant.11.clone.1), kind=kCustom, calls=%fused_computation.185 | custom fusion | flops 1024 | bytes 3145732 | tf_op jit(solution)/shard_map/scatter-add | solution.py:115
  535.2 6.7 fusion.3
  559.6 40.7 %psum.45 = f32[]{:T(128)} all-reduce(f32[]{:T(128)S(6)} %add.657), channel_id=1, replica_groups=mesh['tm'=4,'lon'=8] {'tm','lon'}, use_global_device_ids=true, to_apply=%region_17.18 | all-reduce | flops 1 | bytes 8 | tf_op jit(solution)/shard_map/psum | solution.py:145
  615.2 39.9 %psum.46 = f32[]{:T(128)} all-reduce(f32[]{:T(128)S(6)} %add.660), channel_id=1, replica_groups=mesh['tm'=4,'lon'=8] {'tm','lon'}, use_global_device_ids=true, to_apply=%region_21.22 | all-reduce | flops 1 | bytes 8 | tf_op jit(solution)/shard_map/psum | solution.py:145
  655.8 8.1 %multiply_reduce_fusion = f32[]{:T(128)} fusion(f32[786432]{0:T(1024)} %get-tuple-element.19, f32[]{:T(128)} %psum.46, f32[]{:T(128)S(6)} %div.64, f32[786432]{0:T(1024)} %bitcast.142, f32[]{:T(128)} %psum.45, f32[786432]{0:T(1024)} %scatter_custom_fusion.1, f32[786432]{0:T(1024)} %bitcast.146), kind=kLoop, calls=%fused_computation.155 | loop fusion | flops 7077887 | bytes 12582928 | tf_op jit(solution)/shard_map/reduce_sum | solution.py:130
  673.4 40.7 %psum.47 = f32[]{:T(128)} all-reduce(f32[]{:T(128)S(6)} %add.663), channel_id=1, replica_groups=mesh['tm'=4,'lon'=8] {'tm','lon'}, use_global_device_ids=true, to_apply=%region_25.26 | all-reduce | flops 1 | bytes 8 | tf_op jit(solution)/shard_map/psum | solution.py:148
  (315 shorter events, 285.3 us)
Async XLA Ops:
  63.8 15.1 %collective-permute-start.5 = (f32[3,1024,1]{1,2,0:T(1,128)S(1)}, f32[3,1024,1]{1,2,0:T(1,128)S(1)}, u32[]{:S(2)}, u32[]{:S(2)}) collective-permute-start(f32[3,1024,1]{1,2,0:T(1,128)S(1)} %copy.29), channel_id=1, source_target_pairs={{1,0},{2,1},{3,2},{4,3},{5,4},{6,5},{7,6},{0,7},{9,8},{10,9},{11,1... | collective-permute-start | bytes 36872 | tf_op jit(solution)/shard_map/ppermute | solution.py:24
  66.7 13.8 %collective-permute-start.6 = (f32[3,1024,1]{1,2,0:T(1,128)S(1)}, f32[3,1024,1]{1,2,0:T(1,128)S(1)}, u32[]{:S(2)}, u32[]{:S(2)}) collective-permute-start(f32[3,1024,1]{1,2,0:T(1,128)S(1)} %copy.31), channel_id=1, source_target_pairs={{0,1},{1,2},{2,3},{3,4},{4,5},{5,6},{6,7},{7,0},{8,9},{9,10},{10,1... | collective-permute-start | bytes 36872 | tf_op jit(solution)/shard_map/ppermute | solution.py:23
  66.8 72.9 %collective-permute-start = (f32[3,1024,256]{2,1,0:T(8,128)}, f32[3,1024,256]{2,1,0:T(8,128)}, u32[]{:S(2)}, u32[]{:S(2)}) collective-permute-start(f32[3,1024,256]{2,1,0:T(8,128)} %bitcast.138), channel_id=1, source_target_pairs={{8,0},{16,8},{24,16},{9,1},{17,9},{25,17},{10,2},{18,10},{26,18},{... | collective-permute-start | bytes 9437192 | tf_op jit(solution)/shard_map/ppermute | solution.py:13
  97.4 9.9 %collective-permute-start.7 = (f32[3,1024,1]{1,2,0:T(1,128)S(1)}, f32[3,1024,1]{1,2,0:T(1,128)S(1)}, u32[]{:S(2)}, u32[]{:S(2)}) collective-permute-start(f32[3,1024,1]{1,2,0:T(1,128)S(1)} %copy.33), channel_id=1, source_target_pairs={{1,0},{2,1},{3,2},{4,3},{5,4},{6,5},{7,6},{0,7},{9,8},{10,9},{11,1... | collective-permute-start | bytes 36872 | tf_op jit(solution)/shard_map/ppermute | solution.py:24
  101.9 7.1 collective-permute-start.8
  149.3 7.8 %collective-permute-start.1 = (f32[3,1024,1]{1,2,0:T(1,128)S(1)}, f32[3,1024,1]{1,2,0:T(1,128)S(1)}, u32[]{:S(2)}, u32[]{:S(2)}) collective-permute-start(f32[3,1024,1]{1,2,0:T(1,128)S(1)} %copy.21), channel_id=1, source_target_pairs={{1,0},{2,1},{3,2},{4,3},{5,4},{6,5},{7,6},{0,7},{9,8},{10,9},{11,1... | collective-permute-start | bytes 36872 | tf_op jit(solution)/shard_map/ppermute | solution.py:24
  152.9 5.9 collective-permute-start.2
  178.9 18.0 %copy-start.85 = (f32[1,1024]{1,0:T(1,128)S(1)}, f32[1,1024]{1,0:T(1,128)}, u32[]{:S(2)}) copy-start(f32[1,1024]{1,0:T(1,128)} %param.8) | copy-start | bytes 12292
  178.9 18.1 %copy-start.84 = (f32[1,1024]{1,0:T(1,128)S(1)}, f32[1,1024]{1,0:T(1,128)}, u32[]{:S(2)}) copy-start(f32[1,1024]{1,0:T(1,128)} %param.11) | copy-start | bytes 12292
  178.9 71.6 %collective-permute-start.9 = (f32[3,1024,256]{2,1,0:T(8,128)}, f32[3,1024,256]{2,1,0:T(8,128)}, u32[]{:S(2)}, u32[]{:S(2)}) collective-permute-start(f32[3,1024,256]{2,1,0:T(8,128)} %get-tuple-element.105), channel_id=1, source_target_pairs={{0,8},{8,16},{16,24},{1,9},{9,17},{17,25},{2,10},{10,18},{18,26},{... | collective-permute-start | bytes 9437192 | tf_op jit(solution)/shard_map/ppermute | solution.py:13
  216.0 8.5 %collective-permute-start.3 = (f32[3,1024,1]{1,2,0:T(1,128)S(1)}, f32[3,1024,1]{1,2,0:T(1,128)S(1)}, u32[]{:S(2)}, u32[]{:S(2)}) collective-permute-start(f32[3,1024,1]{1,2,0:T(1,128)S(1)} %copy.25), channel_id=1, source_target_pairs={{1,0},{2,1},{3,2},{4,3},{5,4},{6,5},{7,6},{0,7},{9,8},{10,9},{11,1... | collective-permute-start | bytes 36872 | tf_op jit(solution)/shard_map/ppermute | solution.py:24
  220.3 6.0 collective-permute-start.4
  238.5 11.9 %copy-start.16 = (f32[3,1024,256]{2,1,0:T(8,128)S(1)}, f32[3,1024,256]{2,1,0:T(8,128)}, u32[]{:S(2)}) copy-start(f32[3,1024,256]{2,1,0:T(8,128)} %get-tuple-element.27) | copy-start | bytes 9437188
  367.5 71.4 %collective-permute-start.15 = (f32[3,1024,256]{2,1,0:T(8,128)}, f32[3,1024,256]{2,1,0:T(8,128)}, u32[]{:S(2)}, u32[]{:S(2)}) collective-permute-start(f32[3,1024,256]{2,1,0:T(8,128)} %get-tuple-element.17), channel_id=1, source_target_pairs={{8,0},{16,8},{24,16},{9,1},{17,9},{25,17},{10,2},{18,10},{26,18},{... | collective-permute-start | bytes 9437192 | tf_op jit(solution)/shard_map/ppermute | solution.py:13
  372.8 3.0 collective-permute-start.10
  375.8 4.0 collective-permute-start.11
  396.7 7.8 %collective-permute-start.12 = (f32[3,1024,1]{1,2,0:T(1,128)S(1)}, f32[3,1024,1]{1,2,0:T(1,128)S(1)}, u32[]{:S(2)}, u32[]{:S(2)}) collective-permute-start(f32[3,1024,1]{1,2,0:T(1,128)S(1)} %copy.41), channel_id=1, source_target_pairs={{1,0},{2,1},{3,2},{4,3},{5,4},{6,5},{7,6},{0,7},{9,8},{10,9},{11,1... | collective-permute-start | bytes 36872 | tf_op jit(solution)/shard_map/ppermute | solution.py:24
  398.9 7.3 %collective-permute-start.13 = (f32[3,1024,1]{1,2,0:T(1,128)S(1)}, f32[3,1024,1]{1,2,0:T(1,128)S(1)}, u32[]{:S(2)}, u32[]{:S(2)}) collective-permute-start(f32[3,1024,1]{1,2,0:T(1,128)S(1)} %copy.43), channel_id=1, source_target_pairs={{0,1},{1,2},{2,3},{3,4},{4,5},{5,6},{6,7},{7,0},{8,9},{9,10},{10,1... | collective-permute-start | bytes 36872 | tf_op jit(solution)/shard_map/ppermute | solution.py:23
  448.5 6.7 collective-permute-start.16
  450.5 6.4 collective-permute-start.17
  474.4 71.7 %collective-permute-start.14 = (f32[3,1024,256]{2,1,0:T(8,128)}, f32[3,1024,256]{2,1,0:T(8,128)}, u32[]{:S(2)}, u32[]{:S(2)}) collective-permute-start(f32[3,1024,256]{2,1,0:T(8,128)} %pad_maximum_fusion.46), channel_id=1, source_target_pairs={{0,8},{8,16},{16,24},{1,9},{9,17},{17,25},{2,10},{10,18},{18,26},{... | collective-permute-start | bytes 9437192 | tf_op jit(solution)/shard_map/ppermute | solution.py:13
  523.5 8.3 %collective-permute-start.18 = (f32[3,1024,1]{1,2,0:T(1,128)S(1)}, f32[3,1024,1]{1,2,0:T(1,128)S(1)}, u32[]{:S(2)}, u32[]{:S(2)}) collective-permute-start(f32[3,1024,1]{1,2,0:T(1,128)S(1)} %copy.49), channel_id=1, source_target_pairs={{1,0},{2,1},{3,2},{4,3},{5,4},{6,5},{7,6},{0,7},{9,8},{10,9},{11,1... | collective-permute-start | bytes 36872 | tf_op jit(solution)/shard_map/ppermute | solution.py:24
  527.3 6.2 collective-permute-start.19
  655.8 10.2 %copy-start.18 = (f32[3,1024,256]{2,1,0:T(8,128)S(1)}, f32[3,1024,256]{2,1,0:T(8,128)}, u32[]{:S(2)}) copy-start(f32[3,1024,256]{2,1,0:T(8,128)} %get-tuple-element.23) | copy-start | bytes 9437188
  (83 other events, 396.8 us)
where the time goes:
time: 731 us; the launch traced here: 725 us
  blocking collectives  243 us (33%)
  other arithmetic  224 us (31%)
  local copies, waits for them, and re-layouts  152 us (21%)
  waiting for transfers between devices  56.9 us (8%)
  starting transfers between devices  26.4 us (4%)
  between operations  22.8 us (3%)
    psum x3, blocking collectives, orthogonalize(): coef_value = lax.psum(local_product(vector, image), ('tm', 'lon'))  121 us
    psum x2, blocking collectives, orthogonalize(): remain = lax.psum(local_product(image, image), ('tm', 'lon'))  80 us
    ppermute x4, waiting for transfers between devices, passed_along(): return lax.ppermute(block, axis, route)  54.5 us
    psum x1, blocking collectives, shards(): start_square = lax.psum(local_product(start, start), ('tm', 'lon'))  42 us
    mul x6, other arithmetic, centered_x(): return 0.5 * (extended[:, :, 2:] - extended[:, :, :-2])  39.7 us
    slice x16, local copies, waits for them, and re-layouts, with_halo(): first = lax.slice_in_dim(shard, 0, width, axis=dim)  35.3 us
    unnamed x180, local copies, waits for them, and re-layouts  35.2 us
    mul x8, other arithmetic, walled_y(): return 0.5 * (padded[:, 2:, :] - padded[:, :-2, :])  35 us
  transfers between devices with their start and end apart: 20, of which 5 were waited for; matrix products, arithmetic and copies ran while one was open for 30% of the time, Pallas kernels for 0%

commit v1 on v0

--- a/solution.py
+++ b/solution.py
@@ -142,7 +142,7 @@
 def orthogonalize(image, basis_list):
     coef_list = []
     for vector in basis_list:
-        coef_value = lax.psum(local_product(vector, image), ("tm", "lon"))
+        coef_value = jax.lax.psum(jax.lax.psum(local_product(vector, image), "lon"), "tm")
         image = minus_scaled(image, vector, coef_value)
         coef_list.append(coef_value)
     remain = lax.psum(local_product(image, image), ("tm", "lon"))

time: 731 us -> 680 us (0.930)
  blocking collectives: 243 us -> 191 us
    psum x3 -> x6, blocking collectives: 121 us -> 72.6 us  [the longest x3 41 us: orthogonalize(): jax.lax.psum(local_product(vector, image), 'lon')]
  transfers between devices with their start and end apart: 20 -> 20, of which waited for: 5 -> 5; matrix products, arithmetic and copies ran while one was open for 30% -> 32% of each run, Pallas kernels for 0% -> 0%
where the time goes in v1:
time: 680 us; the launch traced here: 674 us
  other arithmetic  224 us (33%)
  blocking collectives  191 us (28%)
  local copies, waits for them, and re-layouts  152 us (22%)
  waiting for transfers between devices  56.9 us (8%)
  starting transfers between devices  26.6 us (4%)
  between operations  23 us (3%)
    psum x2, blocking collectives, orthogonalize(): remain = lax.psum(local_product(image, image), ('tm', 'lon'))  76.9 us
    ppermute x4, waiting for transfers between devices, passed_along(): return lax.ppermute(block, axis, route)  54.5 us
    psum x1, blocking collectives, shards(): start_square = lax.psum(local_product(start, start), ('tm', 'lon'))  42 us
    psum x3, blocking collectives, orthogonalize(): jax.lax.psum(local_product(vector, image), 'lon')  41 us
    mul x6, other arithmetic, centered_x(): return 0.5 * (extended[:, :, 2:] - extended[:, :, :-2])  39.9 us
    slice x16, local copies, waits for them, and re-layouts, with_halo(): first = lax.slice_in_dim(shard, 0, width, axis=dim)  35.3 us
    unnamed x180, local copies, waits for them, and re-layouts  35.1 us
    mul x8, other arithmetic, walled_y(): return 0.5 * (padded[:, 2:, :] - padded[:, :-2, :])  34.9 us
  transfers between devices with their start and end apart: 20, of which 5 were waited for; matrix products, arithmetic and copies ran while one was open for 32% of the time, Pallas kernels for 0%

profile of v1, /device:TPU:0, one launch (start us, length us, event | category | flops | bytes accessed | tf_op | source)
XLA Modules:
  0.0 673.9 jit_solution(10916087388234075831)
XLA Ops:
  8.8 42.0 %psum.63 = f32[]{:T(128)} all-reduce(f32[]{:T(128)S(6)} %add.572), channel_id=1, replica_groups=mesh['tm'=4,'lon'=8] {'tm','lon'}, use_global_device_ids=true, to_apply=%region_3.0 | all-reduce | flops 1 | bytes 8 | tf_op jit(solution)/shard_map/psum | solution.py:159
  51.5 7.8 %bitcast_subtract_fusion = (f32[3,1024,256]{2,1,0:T(8,128)S(1)}, f32[3,1024,256]{2,1,0:T(8,128)}, f32[1,3,1024,256]{3,2,1,0:T(8,128)S(1)}, f32[1,3,1024,256]{3,2,1,0:T(8,128)}) fusion(f32[1,3,1024,256]{3,2,1,0:T(8,128)} %param.10, f32[1,3,1024,256]{3,2,1,0:T(8,128)} %param.7, f32[]{:T(128)S(6)} %div.60, f32[1,3,1024,256]{3,2,1,0:T(8,128)} %param.13), kind=kLoop, calls=%fused_computation.149 | loop fusion | flops 3145728 | bytes 22020100 | tf_op jit(solution)/shard_map/sub | solution.py:123
  82.1 8.0 %subtract_multiply_fusion.4 = (f32[3,1024,256]{2,1,0:T(8,128)S(1)}, f32[3,1024,256]{2,1,0:T(8,128)S(1)}) fusion(f32[3,1024,256]{2,1,0:T(8,128)} %copy-done.19, f32[3,1024,1]{2,1,0:T(8,128)} %copy.32, f32[3,1024,1]{2,1,0:T(8,128)} %copy.30), kind=kLoop, calls=%fused_computation.171 | loop fusion | flops 4718592 | bytes 9461760 | tf_op jit(solution)/shard_map/mul | solution.py:40
  119.7 20.0 %collective-permute-done = f32[3,1024,256]{2,1,0:T(8,128)} collective-permute-done((f32[3,1024,256]{2,1,0:T(8,128)}, f32[3,1024,256]{2,1,0:T(8,128)}, u32[]{:S(2)}, u32[]{:S(2)}) %collective-permute-start) | collective-permute-done | bytes 3145760 | tf_op jit(solution)/shard_map/ppermute | solution.py:13
  160.4 6.8 %fusion.20 = f32[3,1024,256]{2,1,0:T(8,128)S(1)} fusion(f32[3,1024,1]{2,1,0:T(8,128)} %copy.24, f32[1,1024,256]{2,1,0:T(8,128)} %copy-done.76, f32[1,1024,256]{2,1,0:T(8,128)} %copy-done.77, f32[1,1024,256]{2,1,0:T(8,128)} %copy-done.75, f32[3,1024,1]{2,1,0:T(8,128)} %copy.22), kind=kLoop, calls=%fused_computation.121 | loop fusion | flops 6291456 | bytes 6316032 | tf_op jit(solution)/shard_map/mul | solution.py:35
  184.3 12.5 %gather_fusion = f32[1024]{0:T(1024)S(1)} fusion(f32[786432]{0:T(1024)} %multiply_subtract_fusion.2, s32[1024]{0:T(1024)S(1)} %broadcast_clamp_fusion), kind=kCustom, calls=%fused_computation | custom fusion | bytes 12288 | tf_op jit(solution)/shard_map/gather | solution.py:114
  197.4 7.8 %scatter_custom_fusion = f32[786432]{0:T(1024)} fusion(s32[1024]{0:T(1024)S(1)} %bitcast.166, f32[1024]{0:T(1024)S(1)} %get-tuple-element.25, f32[]{:T(128)} %constant.11.clone.1), kind=kCustom, calls=%fused_computation.187 | custom fusion | flops 1024 | bytes 3145732 | tf_op jit(solution)/shard_map/scatter-add | solution.py:115
  241.5 8.9 %collective-permute-done.9 = f32[3,1024,256]{2,1,0:T(8,128)} collective-permute-done((f32[3,1024,256]{2,1,0:T(8,128)}, f32[3,1024,256]{2,1,0:T(8,128)}, u32[]{:S(2)}, u32[]{:S(2)}) %collective-permute-start.9) | collective-permute-done | bytes 3145760 | tf_op jit(solution)/shard_map/ppermute | solution.py:13
  256.0 13.5 %psum.64 = f32[]{:T(128)} all-reduce(f32[]{:T(128)S(6)} %add.617), channel_id=1, replica_groups=mesh['tm'=4,'lon'=8] {'lon'}, use_global_device_ids=true, to_apply=%region_8.9 | all-reduce | flops 1 | bytes 8 | tf_op jit(solution)/shard_map/psum | solution.py:145
  274.7 11.7 %psum.65 = f32[]{:T(128)} all-reduce(f32[]{:T(128)} %psum.64), channel_id=1, replica_groups=mesh['tm'=4,'lon'=8] {'tm'}, use_global_device_ids=true, to_apply=%region_9.10 | all-reduce | flops 1 | bytes 8 | tf_op jit(solution)/shard_map/psum | solution.py:145
  287.8 7.8 %multiply_reduce_fusion.5 = (f32[]{:T(128)}, f32[786432]{0:T(1024)}) fusion(f32[786432]{0:T(1024)} %bitcast.141, f32[]{:T(128)} %psum.65, f32[786432]{0:T(1024)} %scatter_custom_fusion, f32[786432]{0:T(1024)} %bitcast.153), kind=kLoop, calls=%fused_computation.164 | loop fusion | flops 4718591 | bytes 12582920 | tf_op jit(solution)/shard_map/reduce_sum | solution.py:130
  303.2 37.9 %psum.66 = f32[]{:T(128)} all-reduce(f32[]{:T(128)S(6)} %add.620), channel_id=1, replica_groups=mesh['tm'=4,'lon'=8] {'tm','lon'}, use_global_device_ids=true, to_apply=%region_13.14 | all-reduce | flops 1 | bytes 8 | tf_op jit(solution)/shard_map/psum | solution.py:148
  341.8 9.2 %multiply_subtract_fusion.3 = (f32[3,1024,256]{2,1,0:T(8,128)S(1)}, f32[3,1024,256]{2,1,0:T(8,128)}) fusion(f32[3,1024,256]{2,1,0:T(8,128)} %get-tuple-element.23, f32[]{:T(128)S(6)} %div.64, f32[1,3,1024,256]{3,2,1,0:T(8,128)} %param.10, f32[]{:T(128)} %psum.65, f32[3,1024,256]{2,1,0:T(8,128)} %reshape.519, f32[1,1024,256]{2,1,0:T(8,128)} %copy-done.41, ...), kind=kLoop, calls=%fused_computation.176 | loop fusion | flops 7864320 | bytes 22020104 | tf_op jit(solution)/shard_map/sub | solution.py:123
  364.9 8.1 %subtract_multiply_fusion.1 = (f32[3,1024,256]{2,1,0:T(8,128)S(1)}, f32[3,1024,256]{2,1,0:T(8,128)S(1)}) fusion(f32[3,1024,256]{2,1,0:T(8,128)} %copy-done, f32[3,1024,1]{2,1,0:T(8,128)} %copy.40, f32[3,1024,1]{2,1,0:T(8,128)} %copy.38), kind=kLoop, calls=%fused_computation.162 | loop fusion | flops 4718592 | bytes 9461760 | tf_op jit(solution)/shard_map/mul | solution.py:40
  400.4 22.2 %collective-permute-done.15 = f32[3,1024,256]{2,1,0:T(8,128)} collective-permute-done((f32[3,1024,256]{2,1,0:T(8,128)}, f32[3,1024,256]{2,1,0:T(8,128)}, u32[]{:S(2)}, u32[]{:S(2)}) %collective-permute-start.15) | collective-permute-done | bytes 3145760 | tf_op jit(solution)/shard_map/ppermute | solution.py:13
  442.0 6.7 fusion.6
  475.7 12.5 %gather_fusion.1 = f32[1024]{0:T(1024)S(1)} fusion(f32[786432]{0:T(1024)} %bitcast.147, s32[1024]{0:T(1024)S(1)} %broadcast_clamp_fusion), kind=kCustom, calls=%fused_computation.1 | custom fusion | bytes 12288 | tf_op jit(solution)/shard_map/gather | solution.py:114
  488.8 7.8 %scatter_custom_fusion.1 = f32[786432]{0:T(1024)} fusion(s32[1024]{0:T(1024)S(1)} %bitcast.167, f32[1024]{0:T(1024)S(1)} %get-tuple-element.13, f32[]{:T(128)} %constant.11.clone.1), kind=kCustom, calls=%fused_computation.185 | custom fusion | flops 1024 | bytes 3145732 | tf_op jit(solution)/shard_map/scatter-add | solution.py:115
  538.3 15.1 %psum.67 = f32[]{:T(128)} all-reduce(f32[]{:T(128)S(6)} %add.663), channel_id=1, replica_groups=mesh['tm'=4,'lon'=8] {'lon'}, use_global_device_ids=true, to_apply=%region_18.19 | all-reduce | flops 1 | bytes 8 | tf_op jit(solution)/shard_map/psum | solution.py:145
  558.6 9.9 %psum.68 = f32[]{:T(128)} all-reduce(f32[]{:T(128)} %psum.67), channel_id=1, replica_groups=mesh['tm'=4,'lon'=8] {'tm'}, use_global_device_ids=true, to_apply=%region_19.20 | all-reduce | flops 1 | bytes 8 | tf_op jit(solution)/shard_map/psum | solution.py:145
  582.8 12.3 %psum.69 = f32[]{:T(128)} all-reduce(f32[]{:T(128)S(6)} %add.666), channel_id=1, replica_groups=mesh['tm'=4,'lon'=8] {'lon'}, use_global_device_ids=true, to_apply=%region_23.24 | all-reduce | flops 1 | bytes 8 | tf_op jit(solution)/shard_map/psum | solution.py:145
  595.8 10.0 %psum.70 = f32[]{:T(128)} all-reduce(f32[]{:T(128)} %psum.69), channel_id=1, replica_groups=mesh['tm'=4,'lon'=8] {'tm'}, use_global_device_ids=true, to_apply=%region_24.25 | all-reduce | flops 1 | bytes 8 | tf_op jit(solution)/shard_map/psum | solution.py:145
  606.4 8.1 %multiply_reduce_fusion = f32[]{:T(128)} fusion(f32[786432]{0:T(1024)} %get-tuple-element.19, f32[]{:T(128)} %psum.70, f32[]{:T(128)S(6)} %div.64, f32[786432]{0:T(1024)} %bitcast.142, f32[]{:T(128)} %psum.68, f32[786432]{0:T(1024)} %scatter_custom_fusion.1, f32[786432]{0:T(1024)} %bitcast.146), kind=kLoop, calls=%fused_computation.155 | loop fusion | flops 7077887 | bytes 12582928 | tf_op jit(solution)/shard_map/reduce_sum | solution.py:130
  623.6 39.0 %psum.71 = f32[]{:T(128)} all-reduce(f32[]{:T(128)S(6)} %add.669), channel_id=1, replica_groups=mesh['tm'=4,'lon'=8] {'tm','lon'}, use_global_device_ids=true, to_apply=%region_28.29 | all-reduce | flops 1 | bytes 8 | tf_op jit(solution)/shard_map/psum | solution.py:148
  (318 shorter events, 305.3 us)
Async XLA Ops:
  63.8 14.9 %collective-permute-start.5 = (f32[3,1024,1]{1,2,0:T(1,128)S(1)}, f32[3,1024,1]{1,2,0:T(1,128)S(1)}, u32[]{:S(2)}, u32[]{:S(2)}) collective-permute-start(f32[3,1024,1]{1,2,0:T(1,128)S(1)} %copy.29), channel_id=1, source_target_pairs={{1,0},{2,1},{3,2},{4,3},{5,4},{6,5},{7,6},{0,7},{9,8},{10,9},{11,1... | collective-permute-start | bytes 36872 | tf_op jit(solution)/shard_map/ppermute | solution.py:24
  66.8 13.6 %collective-permute-start.6 = (f32[3,1024,1]{1,2,0:T(1,128)S(1)}, f32[3,1024,1]{1,2,0:T(1,128)S(1)}, u32[]{:S(2)}, u32[]{:S(2)}) collective-permute-start(f32[3,1024,1]{1,2,0:T(1,128)S(1)} %copy.31), channel_id=1, source_target_pairs={{0,1},{1,2},{2,3},{3,4},{4,5},{5,6},{6,7},{7,0},{8,9},{9,10},{10,1... | collective-permute-start | bytes 36872 | tf_op jit(solution)/shard_map/ppermute | solution.py:23
  66.8 72.9 %collective-permute-start = (f32[3,1024,256]{2,1,0:T(8,128)}, f32[3,1024,256]{2,1,0:T(8,128)}, u32[]{:S(2)}, u32[]{:S(2)}) collective-permute-start(f32[3,1024,256]{2,1,0:T(8,128)} %bitcast.138), channel_id=1, source_target_pairs={{8,0},{16,8},{24,16},{9,1},{17,9},{25,17},{10,2},{18,10},{26,18},{... | collective-permute-start | bytes 9437192 | tf_op jit(solution)/shard_map/ppermute | solution.py:13
  97.2 10.3 %collective-permute-start.7 = (f32[3,1024,1]{1,2,0:T(1,128)S(1)}, f32[3,1024,1]{1,2,0:T(1,128)S(1)}, u32[]{:S(2)}, u32[]{:S(2)}) collective-permute-start(f32[3,1024,1]{1,2,0:T(1,128)S(1)} %copy.33), channel_id=1, source_target_pairs={{1,0},{2,1},{3,2},{4,3},{5,4},{6,5},{7,6},{0,7},{9,8},{10,9},{11,1... | collective-permute-start | bytes 36872 | tf_op jit(solution)/shard_map/ppermute | solution.py:24
  101.7 7.4 %collective-permute-start.8 = (f32[3,1024,1]{1,2,0:T(1,128)S(1)}, f32[3,1024,1]{1,2,0:T(1,128)S(1)}, u32[]{:S(2)}, u32[]{:S(2)}) collective-permute-start(f32[3,1024,1]{1,2,0:T(1,128)S(1)} %copy.35), channel_id=1, source_target_pairs={{0,1},{1,2},{2,3},{3,4},{4,5},{5,6},{6,7},{7,0},{8,9},{9,10},{10,1... | collective-permute-start | bytes 36872 | tf_op jit(solution)/shard_map/ppermute | solution.py:23
  149.3 7.8 %collective-permute-start.1 = (f32[3,1024,1]{1,2,0:T(1,128)S(1)}, f32[3,1024,1]{1,2,0:T(1,128)S(1)}, u32[]{:S(2)}, u32[]{:S(2)}) collective-permute-start(f32[3,1024,1]{1,2,0:T(1,128)S(1)} %copy.21), channel_id=1, source_target_pairs={{1,0},{2,1},{3,2},{4,3},{5,4},{6,5},{7,6},{0,7},{9,8},{10,9},{11,1... | collective-permute-start | bytes 36872 | tf_op jit(solution)/shard_map/ppermute | solution.py:24
  152.8 5.9 collective-permute-start.2
  174.1 10.1 %copy-start.86 = (s32[1,1024]{1,0:T(1,128)S(1)}, s32[1,1024]{1,0:T(1,128)}, u32[]{:S(2)}) copy-start(s32[1,1024]{1,0:T(1,128)} %param.12) | copy-start | bytes 12292
  178.8 18.0 %copy-start.85 = (f32[1,1024]{1,0:T(1,128)S(1)}, f32[1,1024]{1,0:T(1,128)}, u32[]{:S(2)}) copy-start(f32[1,1024]{1,0:T(1,128)} %param.8) | copy-start | bytes 12292
  178.8 18.0 %copy-start.84 = (f32[1,1024]{1,0:T(1,128)S(1)}, f32[1,1024]{1,0:T(1,128)}, u32[]{:S(2)}) copy-start(f32[1,1024]{1,0:T(1,128)} %param.11) | copy-start | bytes 12292
  178.8 71.6 %collective-permute-start.9 = (f32[3,1024,256]{2,1,0:T(8,128)}, f32[3,1024,256]{2,1,0:T(8,128)}, u32[]{:S(2)}, u32[]{:S(2)}) collective-permute-start(f32[3,1024,256]{2,1,0:T(8,128)} %get-tuple-element.105), channel_id=1, source_target_pairs={{0,8},{8,16},{16,24},{1,9},{9,17},{17,25},{2,10},{10,18},{18,26},{... | collective-permute-start | bytes 9437192 | tf_op jit(solution)/shard_map/ppermute | solution.py:13
  215.9 8.5 %collective-permute-start.3 = (f32[3,1024,1]{1,2,0:T(1,128)S(1)}, f32[3,1024,1]{1,2,0:T(1,128)S(1)}, u32[]{:S(2)}, u32[]{:S(2)}) collective-permute-start(f32[3,1024,1]{1,2,0:T(1,128)S(1)} %copy.25), channel_id=1, source_target_pairs={{1,0},{2,1},{3,2},{4,3},{5,4},{6,5},{7,6},{0,7},{9,8},{10,9},{11,1... | collective-permute-start | bytes 36872 | tf_op jit(solution)/shard_map/ppermute | solution.py:24
  220.1 6.0 collective-permute-start.4
  238.4 12.0 %copy-start.16 = (f32[3,1024,256]{2,1,0:T(8,128)S(1)}, f32[3,1024,256]{2,1,0:T(8,128)}, u32[]{:S(2)}) copy-start(f32[3,1024,256]{2,1,0:T(8,128)} %get-tuple-element.27) | copy-start | bytes 9437188
  351.0 71.5 %collective-permute-start.15 = (f32[3,1024,256]{2,1,0:T(8,128)}, f32[3,1024,256]{2,1,0:T(8,128)}, u32[]{:S(2)}, u32[]{:S(2)}) collective-permute-start(f32[3,1024,256]{2,1,0:T(8,128)} %get-tuple-element.17), channel_id=1, source_target_pairs={{8,0},{16,8},{24,16},{9,1},{17,9},{25,17},{10,2},{18,10},{26,18},{... | collective-permute-start | bytes 9437192 | tf_op jit(solution)/shard_map/ppermute | solution.py:13
  356.2 3.0 collective-permute-start.10
  359.2 4.0 collective-permute-start.11
  380.0 8.0 %collective-permute-start.12 = (f32[3,1024,1]{1,2,0:T(1,128)S(1)}, f32[3,1024,1]{1,2,0:T(1,128)S(1)}, u32[]{:S(2)}, u32[]{:S(2)}) collective-permute-start(f32[3,1024,1]{1,2,0:T(1,128)S(1)} %copy.41), channel_id=1, source_target_pairs={{1,0},{2,1},{3,2},{4,3},{5,4},{6,5},{7,6},{0,7},{9,8},{10,9},{11,1... | collective-permute-start | bytes 36872 | tf_op jit(solution)/shard_map/ppermute | solution.py:24
  382.2 7.5 %collective-permute-start.13 = (f32[3,1024,1]{1,2,0:T(1,128)S(1)}, f32[3,1024,1]{1,2,0:T(1,128)S(1)}, u32[]{:S(2)}, u32[]{:S(2)}) collective-permute-start(f32[3,1024,1]{1,2,0:T(1,128)S(1)} %copy.43), channel_id=1, source_target_pairs={{0,1},{1,2},{2,3},{3,4},{4,5},{5,6},{6,7},{7,0},{8,9},{9,10},{10,1... | collective-permute-start | bytes 36872 | tf_op jit(solution)/shard_map/ppermute | solution.py:23
  432.1 6.6 collective-permute-start.16
  434.0 6.4 collective-permute-start.17
  458.1 71.8 %collective-permute-start.14 = (f32[3,1024,256]{2,1,0:T(8,128)}, f32[3,1024,256]{2,1,0:T(8,128)}, u32[]{:S(2)}, u32[]{:S(2)}) collective-permute-start(f32[3,1024,256]{2,1,0:T(8,128)} %pad_maximum_fusion.46), channel_id=1, source_target_pairs={{0,8},{8,16},{16,24},{1,9},{9,17},{17,25},{2,10},{10,18},{18,26},{... | collective-permute-start | bytes 9437192 | tf_op jit(solution)/shard_map/ppermute | solution.py:13
  507.6 8.0 %collective-permute-start.18 = (f32[3,1024,1]{1,2,0:T(1,128)S(1)}, f32[3,1024,1]{1,2,0:T(1,128)S(1)}, u32[]{:S(2)}, u32[]{:S(2)}) collective-permute-start(f32[3,1024,1]{1,2,0:T(1,128)S(1)} %copy.49), channel_id=1, source_target_pairs={{1,0},{2,1},{3,2},{4,3},{5,4},{6,5},{7,6},{0,7},{9,8},{10,9},{11,1... | collective-permute-start | bytes 36872 | tf_op jit(solution)/shard_map/ppermute | solution.py:24
  511.3 6.0 collective-permute-start.19
  (83 other events, 396.8 us)
